TPU v7x, 32 devices: a whole 2x2x4 slice. The times are simulated.
32 devices in a mesh: gx: 8 (over z, x), gy: 4 (over y, core).
Axes of the slice: x: 2, y: 2, z: 4, core: 2. Of those that a mesh axis runs over, the one named last changes fastest.
Arguments:
- design: float32 [128, 256, 512], P('gx', 'gy'), may hold values from 0 to 1, as said below
- sensitivity: float32 [128, 256, 512], P('gx', 'gy'), may hold values from 0.1 to 10
- solid_mask: int32 [128, 256, 512], P('gx', 'gy'), may hold values 0 or 1
Outputs:
- new_design: float32 [128, 256, 512], P('gx', 'gy')
- objective_grad: float32 [128, 256, 512], P('gx', 'gy')
- multiplier: float32 [], replicated
Inputs may be any that keep to these rules, and one draw needn't show every extreme that they name: design densities lie strictly between 0 and 1.
All inputs are finite; a program needn't handle non-finite values. No bound on the sum of `solid_mask` on one device may be relied on, other than what follows from the above.
Results may differ from a plain program's by a relative error of at most 0.0003.
Values sent between devices are 32-bit elements; how exact they have to be, the bound alone decides.
A program may use at most 64 MiB of HBM per device.

v0:
```python
import functools
import math

import jax
import jax.numpy as jnp
from jax import lax
from jax.experimental import pallas as pl
from jax.experimental.pallas import tpu as pltpu
from jax.sharding import PartitionSpec as P

RADIUS = 8
DUAL_ITERS = 2
SPAN = RADIUS + 1
MESH = pl.DeviceIdType.MESH

beta_value = 4.0
eta_value = 0.5
volume_share = 0.4
move_limit = 0.2
asym_gap = 0.5
TANH_MID = math.tanh(beta_value * eta_value)
SCALE = math.tanh(beta_value * eta_value) + math.tanh(beta_value * (1.0 - eta_value))


def missing(distance):
    out = jnp.maximum(RADIUS - distance, 0)
    return (out * (out + 1)) // 2


def cover(cell, total):
    return (SPAN * SPAN - missing(cell) - missing(total - 1 - cell)).astype(jnp.float32)


def split2(x):
    hi = x.astype(jnp.bfloat16)
    lo = (x - hi.astype(jnp.float32)).astype(jnp.bfloat16)
    return hi, lo


def filter_zy(src, dst, group):
    rows, wide, depth = src.shape
    ry = wide - 2 * RADIUS
    jj = lax.broadcasted_iota(jnp.int32, (ry, wide), 0)
    bb = lax.broadcasted_iota(jnp.int32, (ry, wide), 1)
    band_y = jnp.maximum(SPAN - jnp.abs(jj + RADIUS - bb), 0).astype(jnp.float32).astype(jnp.bfloat16)
    cc = lax.broadcasted_iota(jnp.int32, (depth, depth), 0)
    kk = lax.broadcasted_iota(jnp.int32, (depth, depth), 1)
    band_z = jnp.maximum(SPAN - jnp.abs(cc - kk), 0).astype(jnp.float32).astype(jnp.bfloat16)

    def body(g, carry):
        his, los = [], []
        for r in range(group):
            hi, lo = split2(src[g * group + r])
            out = jnp.dot(band_y, hi, preferred_element_type=jnp.float32) + jnp.dot(
                band_y, lo, preferred_element_type=jnp.float32
            )
            hi, lo = split2(out)
            his.append(hi)
            los.append(lo)
        both = jnp.dot(
            jnp.concatenate(his + los, 0), band_z, preferred_element_type=jnp.float32
        )
        half = group * ry
        total = both[:half] + both[half:]
        for r in range(group):
            dst[g * group + r] = total[r * ry : (r + 1) * ry]
        return carry

    lax.fori_loop(0, rows // group, body, 0)


def filter_x(src, tile, emit):
    count = src.shape[0] - 2 * RADIUS
    load = lambda i: src[i, tile, :]
    box = load(0)
    for k in range(1, SPAN):
        box = box + load(k)
    window = [box]
    for n in range(1, SPAN):
        box = box + (load(n + RADIUS) - load(n - 1))
        window.append(box)
    total = window[0]
    for k in range(1, SPAN):
        total = total + window[k]
    emit(0, total)
    for i in range(1, count):
        n = i + RADIUS
        box = box + (load(n + RADIUS) - load(n - 1))
        total = total + (box - window[i - 1])
        window.append(box)
        emit(i, total)


(DES_UP, DES_DN, MASK, SENS, AFLD, A_UP, A_DN, V_UP, V_DN, O_UP, O_DN, VB, OB,
 VY_UP, VY_DN, OY_UP, OY_DN, COUNT) = range(18)


def kernel(design, sens, mask, obj_out, vol_out, phys_out, dbuf, afull, abuf, mbuf, sbuf, vbuf, obuf,
           vx, ox, vback, oback, send_sems, recv_sems, local_sems):
    rows, ry, depth = design.shape
    half = depth // 2
    gx, gy = lax.axis_index("gx"), lax.axis_index("gy")
    nx, ny = lax.axis_size("gx"), lax.axis_size("gy")
    par = lax.rem(gx, 2)
    pair = gx // 2
    partner = gx + 1 - 2 * par
    has_xl, has_xr = gx >= 2, gx < nx - 2
    has_yl, has_yr = gy >= 1, gy < ny - 1
    xl, xr, yl, yr = (gx - 2, gy), (gx + 2, gy), (gx, gy - 1), (gx, gy + 1)
    mate = (partner, gy)

    barrier = pltpu.get_barrier_semaphore()

    def greet(dev):
        pl.semaphore_signal(barrier, inc=1, device_id=dev, device_id_type=MESH)

    greet(mate)
    for cond, dev in ((has_xl, xl), (has_xr, xr), (has_yl, yl), (has_yr, yr)):
        pl.when(cond)(functools.partial(greet, dev))

    own = pl.ds(pl.multiple_of(par * half, 128), half)
    other = pl.ds(pl.multiple_of((1 - par) * half, 128), half)
    my_rows = pl.ds(par * rows, rows)
    mate_rows = pl.ds((1 - par) * rows, rows)
    mid = pl.ds(RADIUS, ry)

    l_des = pltpu.make_async_copy(design, dbuf.at[:, mid, :], local_sems.at[0])
    l_mask = pltpu.make_async_copy(mask.at[:, :, own], mbuf.at[my_rows], local_sems.at[1])
    l_sens = pltpu.make_async_copy(sens.at[:, :, own], sbuf.at[my_rows], local_sems.at[2])
    l_des.start()
    l_mask.start()
    l_sens.start()

    count = 1 + sum(c.astype(jnp.int32) for c in (has_xl, has_xr, has_yl, has_yr))
    pl.semaphore_wait(barrier, count)

    def remote(idx, src, dst, dev):
        return pltpu.make_async_remote_copy(
            src_ref=src, dst_ref=dst, send_sem=send_sems.at[idx], recv_sem=recv_sems.at[idx],
            device_id=dev, device_id_type=MESH,
        )

    def y_pair(up, dn, src, off, buf):
        return (
            remote(up, src.at[:, pl.ds(off + ry - RADIUS, RADIUS), :], buf.at[:, pl.ds(0, RADIUS), :], yr),
            remote(dn, src.at[:, pl.ds(off, RADIUS), :], buf.at[:, pl.ds(RADIUS + ry, RADIUS), :], yl),
        )

    def x_pair(up, dn, buf):
        return (
            remote(up, buf.at[pl.ds(2 * rows, RADIUS)], buf.at[pl.ds(0, RADIUS)], xr),
            remote(dn, buf.at[pl.ds(RADIUS, RADIUS)], buf.at[pl.ds(RADIUS + 2 * rows, RADIUS)], xl),
        )

    def begin(two, low, high):
        pl.when(high)(lambda: two[0].start())
        pl.when(low)(lambda: two[1].start())

    def finish(two, low, high):
        pl.when(low)(lambda: two[0].wait_recv())
        pl.when(high)(lambda: two[1].wait_recv())

    def sent(two, low, high):
        pl.when(high)(lambda: two[0].wait_send())
        pl.when(low)(lambda: two[1].wait_send())

    r_des = y_pair(DES_UP, DES_DN, design, 0, dbuf)
    begin(r_des, has_yl, has_yr)
    r_mask = remote(MASK, mask.at[:, :, other], mbuf.at[my_rows], mate)
    r_mask.start()

    def zero_y(buf):
        zero = jnp.zeros((rows, RADIUS, depth), jnp.float32)

        @pl.when(jnp.logical_not(has_yl))
        def _():
            buf[:, 0:RADIUS, :] = zero

        @pl.when(jnp.logical_not(has_yr))
        def _():
            buf[:, RADIUS + ry :, :] = zero

    def zero_x(buf):
        zero = jnp.zeros((RADIUS, ry, half), jnp.float32)

        @pl.when(jnp.logical_not(has_xl))
        def _():
            buf[0:RADIUS] = zero

        @pl.when(jnp.logical_not(has_xr))
        def _():
            buf[RADIUS + 2 * rows :] = zero

    for buf in (dbuf, vback, oback):
        zero_y(buf)
    for buf in (abuf, vbuf, obuf):
        zero_x(buf)

    group = 4 if rows % 4 == 0 else 1
    l_des.wait()
    finish(r_des, has_yl, has_yr)
    filter_zy(dbuf, afull, group)
    r_a = remote(AFLD, afull.at[:, :, other], abuf.at[pl.ds(RADIUS + par * rows, rows)], mate)
    r_a.start()
    r_sens = remote(SENS, sens.at[:, :, other], sbuf.at[my_rows], mate)
    r_sens.start()
    l_a = pltpu.make_async_copy(afull.at[:, :, own], abuf.at[pl.ds(RADIUS + par * rows, rows)], local_sems.at[3])
    l_a.start()
    l_a.wait()
    r_a.wait_recv()
    x_a = x_pair(A_UP, A_DN, abuf)
    begin(x_a, has_xl, has_xr)
    l_mask.wait()
    r_mask.wait_recv()
    finish(x_a, has_xl, has_xr)

    total_x, total_y = rows * nx, ry * ny
    wz = cover(par * half + lax.broadcasted_iota(jnp.int32, (8, half), 1), depth)

    phys_out[...] = jnp.zeros_like(phys_out)

    def stage_one(j, carry):
        tile = pl.ds(pl.multiple_of(j * 8, 8), 8)
        wy = cover(gy * ry + j * 8 + lax.broadcasted_iota(jnp.int32, (8, half), 0), total_y)
        wyz = wy * wz

        def emit(i, value):
            weight = wyz * cover(pair * (2 * rows) + i, total_x)
            inv = 1.0 / weight
            shifted = jnp.tanh(beta_value * (value * inv - eta_value))
            solid = mbuf[i, tile, :]
            free = (1 - solid).astype(jnp.float32)
            phys_out[...] += jnp.where(solid == 1, 1.0, (TANH_MID + shifted) * (1.0 / SCALE))
            vbuf[RADIUS + i, tile, :] = (beta_value / SCALE) * (1.0 - shifted * shifted) * free * inv

        filter_x(abuf, tile, emit)
        return carry

    lax.fori_loop(0, ry // 8, stage_one, 0)
    x_v = x_pair(V_UP, V_DN, vbuf)
    begin(x_v, has_xl, has_xr)
    finish(x_v, has_xl, has_xr)

    def x_only(src, dst):
        def body(j, carry):
            tile = pl.ds(pl.multiple_of(j * 8, 8), 8)

            def emit(i, value):
                dst[i, tile, :] = value

            filter_x(src, tile, emit)
            return carry

        lax.fori_loop(0, ry // 8, body, 0)

    x_only(vbuf, vx)
    r_vb = remote(VB, vx.at[mate_rows], vback.at[:, mid, own], mate)
    r_vb.start()
    l_vb = pltpu.make_async_copy(vx.at[my_rows], vback.at[:, mid, own], local_sems.at[4])
    l_vb.start()

    l_sens.wait()
    r_sens.wait_recv()

    def times(i, carry):
        obuf[RADIUS + i] = -sbuf[i] * vbuf[RADIUS + i]
        return carry

    lax.fori_loop(0, 2 * rows, times, 0)
    x_o = x_pair(O_UP, O_DN, obuf)
    begin(x_o, has_xl, has_xr)
    finish(x_o, has_xl, has_xr)
    x_only(obuf, ox)
    r_ob = remote(OB, ox.at[mate_rows], oback.at[:, mid, own], mate)
    r_ob.start()
    l_ob = pltpu.make_async_copy(ox.at[my_rows], oback.at[:, mid, own], local_sems.at[5])
    l_ob.start()

    l_vb.wait()
    r_vb.wait_recv()
    y_v = y_pair(VY_UP, VY_DN, vback, RADIUS, vback)
    begin(y_v, has_yl, has_yr)
    finish(y_v, has_yl, has_yr)
    filter_zy(vback, vol_out, group)

    l_ob.wait()
    r_ob.wait_recv()
    y_o = y_pair(OY_UP, OY_DN, oback, RADIUS, oback)
    begin(y_o, has_yl, has_yr)
    finish(y_o, has_yl, has_yr)
    filter_zy(oback, obj_out, group)

    for one in (r_mask, r_a, r_sens, r_vb, r_ob):
        one.wait_send()
    for two in (r_des, y_v, y_o):
        sent(two, has_yl, has_yr)
    for two in (x_a, x_v, x_o):
        sent(two, has_xl, has_xr)


def gradients(design, sensitivity, solid_mask):
    rows, ry, depth = design.shape
    half = depth // 2
    f32 = jnp.float32
    wide = (rows, ry + 2 * RADIUS, depth)
    tall = (2 * rows + 2 * RADIUS, ry, half)
    strip = (2 * rows, ry, half)
    vmem = pl.BlockSpec(memory_space=pltpu.VMEM)
    return pl.pallas_call(
        kernel,
        out_shape=(
            jax.ShapeDtypeStruct((rows, ry, depth), f32),
            jax.ShapeDtypeStruct((rows, ry, depth), f32),
            jax.ShapeDtypeStruct((8, half), f32),
        ),
        in_specs=[pl.BlockSpec(memory_space=pl.ANY)] * 3,
        out_specs=(vmem, vmem, vmem),
        scratch_shapes=[
            pltpu.VMEM(wide, f32),
            pltpu.VMEM((rows, ry, depth), f32),
            pltpu.VMEM(tall, f32),
            pltpu.VMEM(strip, jnp.int32),
            pltpu.VMEM(strip, f32),
            pltpu.VMEM(tall, f32),
            pltpu.VMEM(tall, f32),
            pltpu.VMEM(strip, f32),
            pltpu.VMEM(strip, f32),
            pltpu.VMEM(wide, f32),
            pltpu.VMEM(wide, f32),
            pltpu.SemaphoreType.DMA((COUNT,)),
            pltpu.SemaphoreType.DMA((COUNT,)),
            pltpu.SemaphoreType.DMA((6,)),
        ],
        compiler_params=pltpu.CompilerParams(
            collective_id=0, has_side_effects=True, vmem_limit_bytes=56 * 1024 * 1024
        ),
    )(design, sensitivity, solid_mask)


def dual_point(lam, design, p_zero, q_zero, p_one, q_one, lower, upper):
    low = design - asym_gap
    upp = design + asym_gap
    a_root = jnp.sqrt(p_zero + lam * p_one)
    b_root = jnp.sqrt(q_zero + lam * q_one)
    raw = (a_root * low + b_root * upp) / (a_root + b_root)
    inside = jnp.logical_and(raw > lower, raw < upper).astype(jnp.float32)
    point = jnp.clip(raw, lower, upper)
    value = p_one / (upp - point) + q_one / (point - low)
    moved = (
        (upp - low)
        * (a_root * q_one / (2.0 * b_root) - b_root * p_one / (2.0 * a_root))
        / (a_root + b_root) ** 2
    )
    change = (p_one / (upp - point) ** 2 - q_one / (point - low) ** 2) * inside * moved
    return (point, value, change)


def per_device(design, sensitivity, solid_mask):
    rows_x, rows_y, depth = design.shape
    cell_count = float(rows_x * rows_y * depth * lax.axis_size("gx") * lax.axis_size("gy"))
    objective_grad, volume_grad, phys = gradients(design, sensitivity, solid_mask)
    free = (1 - solid_mask).astype(jnp.float32)
    p_zero = 0.25 * (
        1.001 * jnp.maximum(objective_grad, 0.0) + 0.001 * jnp.maximum(-objective_grad, 0.0) + 1e-05
    )
    q_zero = 0.25 * (
        0.001 * jnp.maximum(objective_grad, 0.0) + 1.001 * jnp.maximum(-objective_grad, 0.0) + 1e-05
    )
    p_one = 0.25 * 1.001 * volume_grad * free
    q_one = 0.25 * 0.001 * volume_grad * free
    lower = jnp.maximum(0.0, design - move_limit)
    upper = jnp.minimum(1.0, design + move_limit)
    base_local = jnp.sum((p_one + q_one) / asym_gap)
    mass_local = jnp.sum(phys) - volume_share * rows_x * rows_y * depth
    lam = jnp.float32(1.0)
    base_total, mass_total = lax.psum((base_local, mass_local), ("gx", "gy"))
    offset = mass_total / cell_count - base_total / cell_count
    for turn in range(DUAL_ITERS):
        point, value, change = dual_point(lam, design, p_zero, q_zero, p_one, q_one, lower, upper)
        value_total, change_total = lax.psum((jnp.sum(value), jnp.sum(change)), ("gx", "gy"))
        level = value_total / cell_count + offset
        rate = change_total / cell_count
        lam = lam * jnp.exp(-level / (lam * rate - 1e-06))
    point, value, change = dual_point(lam, design, p_zero, q_zero, p_one, q_one, lower, upper)
    new_design = jnp.where(solid_mask == 1, design, point)
    return (new_design, objective_grad, lam)


def solution(mesh):
    return jax.shard_map(
        per_device,
        mesh=mesh,
        in_specs=(P("gx", "gy", None), P("gx", "gy", None), P("gx", "gy", None)),
        out_specs=(P("gx", "gy", None), P("gx", "gy", None), P()),
        check_vma=False,
    )
```

profile of v0, /device:TPU:0, one launch (start us, length us, event | category | flops | bytes accessed | tf_op | source)
XLA Modules:
  0.0 248.8 jit_solution(16790886255167946220)
XLA Ops:
  0.6 0.0 copy-start
  0.6 0.0 copy-start.2
  0.7 129.0 %shard_map.58 = (f32[16,64,512]{2,1,0:T(8,128)}, f32[16,64,512]{2,1,0:T(8,128)}, f32[8,256]{1,0:T(8,128)}) custom-call(f32[16,64,512]{2,1,0:T(8,128)} %design.1, f32[16,64,512]{2,1,0:T(8,128)} %sens.1, s32[16,64,512]{2,1,0:T(8,128)} %mask.1), custom_call_target="tpu_custom_call" | custom-call | tf_op jit(solution)/shard_map/pallas_call | solution.py:309
  129.6 0.0 copy-done
  129.6 0.0 copy-done.2
  129.6 0.0 copy-start.3
  129.7 9.4 %multiply_reduce_fusion.1 = (f32[]{:T(128)}, f32[]{:T(128)}, f32[]{:T(128)}, f32[16,64,512]{2,1,0:T(8,128)}, f32[16,64,512]{2,1,0:T(8,128)}) fusion(f32[16,64,512]{2,1,0:T(8,128)S(1)} %copy-done, f32[16,64,512]{2,1,0:T(8,128)} %get-tuple-element.26, s32[16,64,512]{2,1,0:T(8,128)S(1)} %copy-done.2, f32[16,64,512]{2,1,0:T(8,128)} %get-tuple-element.7), kind=kLoop, calls=%fused_computation.7 | loop fusion | flops 34078720 | bytes 12582924 | tf_op jit(solution)/shard_map/reduce_sum | solution.py:380
  139.1 0.0 copy-done.3
  139.1 0.6 reduce_sum.55
  140.3 48.0 %all-reduce.1 = (f32[]{:T(128)}, f32[]{:T(128)}, f32[]{:T(128)}, f32[]{:T(128)}) all-reduce(f32[]{:T(128)} %get-tuple-element.12, f32[]{:T(128)S(6)} %sub.60, f32[]{:T(128)} %get-tuple-element.13, f32[]{:T(128)} %get-tuple-element.11), channel_id=1, replica_groups=mesh['gx'=8,'gy'=4] {'gx','gy'}, use_global_device_ids=true, to_apply=%region_1.0 | all-reduce | flops 4 | bytes 32 | tf_op jit(solution)/shard_map/psum | solution.py:380
  190.9 7.9 %multiply_reduce_fusion = (f32[]{:T(128)}, f32[]{:T(128)}) fusion(f32[16,64,512]{2,1,0:T(8,128)} %get-tuple-element.20, f32[16,64,512]{2,1,0:T(8,128)} %get-tuple-element.21, f32[16,64,512]{2,1,0:T(8,128)S(1)} %copy-done, f32[]{:T(128)S(6)} %exp.6, f32[16,64,512]{2,1,0:T(8,128)} %get-tuple-element.26), kind=kLoop, calls=%fused_computation.1 | loop fusion | flops 30408704 | bytes 8388620 | tf_op jit(solution)/shard_map/reduce_sum | solution.py:380
  198.8 39.0 %all-reduce = (f32[]{:T(128)}, f32[]{:T(128)}) all-reduce(f32[]{:T(128)} %get-tuple-element.10, f32[]{:T(128)} %get-tuple-element.9), channel_id=1, replica_groups=mesh['gx'=8,'gy'=4] {'gx','gy'}, use_global_device_ids=true, to_apply=%region_9.10 | all-reduce | flops 2 | bytes 16 | tf_op jit(solution)/shard_map/psum | solution.py:380
  239.2 0.0 copy-start.1
  239.2 7.2 %minimum_select_fusion = f32[16,64,512]{2,1,0:T(8,128)} fusion(f32[16,64,512]{2,1,0:T(8,128)S(1)} %copy-done, f32[16,64,512]{2,1,0:T(8,128)} %get-tuple-element.21, f32[16,64,512]{2,1,0:T(8,128)} %get-tuple-element.20, s32[16,64,512]{2,1,0:T(8,128)} %mask.1, f32[]{:T(128)} %mul.156, f32[16,64,512]{2,1,0:T(8,128)} %get-tuple-element.26), kind=kLoop, calls=%fused_computation | loop fusion | flops 16777216 | bytes 12582916 | tf_op jit(solution)/shard_map/jit(_where)/select_n | solution.py:385
  246.4 0.0 copy-done.1
  246.4 1.3 copy.7
Async XLA Ops:
  0.6 129.0 %copy-start = (f32[16,64,512]{2,1,0:T(8,128)S(1)}, f32[16,64,512]{2,1,0:T(8,128)}, u32[]{:S(2)}) copy-start(f32[16,64,512]{2,1,0:T(8,128)} %design.1) | copy-start | bytes 6291460
  0.6 129.0 %copy-start.2 = (s32[16,64,512]{2,1,0:T(8,128)S(1)}, s32[16,64,512]{2,1,0:T(8,128)}, u32[]{:S(2)}) copy-start(s32[16,64,512]{2,1,0:T(8,128)} %mask.1) | copy-start | bytes 6291460
  129.6 9.4 %copy-start.3 = (f32[8,256]{1,0:T(8,128)S(1)}, f32[8,256]{1,0:T(8,128)}, u32[]{:S(2)}) copy-start(f32[8,256]{1,0:T(8,128)} %get-tuple-element.8) | copy-start | bytes 24580
  239.2 7.2 %copy-start.1 = (f32[16,64,512]{2,1,0:T(8,128)S(1)}, f32[16,64,512]{2,1,0:T(8,128)}, u32[]{:S(2)}) copy-start(f32[16,64,512]{2,1,0:T(8,128)} %get-tuple-element.26) | copy-start | bytes 6291460
where the time goes:
time: 249 us
  Pallas kernels  129 us (52%)
  blocking collectives  87.1 us (35%)
  other arithmetic  25.1 us (10%)
  between operations  6.37 us (3%)
    pallas_call x1, Pallas kernels, gradients(): pl.pallas_call(kernel, out_shape=(jax.ShapeDtypeStruct((rows, ry, depth),...  129 us
    psum x2, blocking collectives, per_device(): lax.psum((jnp.sum(value), jnp.sum(change)), ('gx', 'gy'))  87.1 us
    reduce_sum x2, other arithmetic, per_device(): jnp.sum(change)  17.3 us
    select_n x1, other arithmetic, per_device(): new_design = jnp.where(solid_mask == 1, design, point)  7.17 us

commit v1 on v0

--- a/solution.py
+++ b/solution.py
@@ -95,8 +95,9 @@
  VY_UP, VY_DN, OY_UP, OY_DN, COUNT) = range(18)
 
 
-def kernel(design, sens, mask, obj_out, vol_out, phys_out, dbuf, afull, abuf, mbuf, sbuf, vbuf, obuf,
-           vx, ox, vback, oback, send_sems, recv_sems, local_sems):
+def kernel(design, sens, mask, new_out, obj_out, lam_out, vol_out, phys_out, full_mask, dbuf, afull, abuf, mbuf,
+           sbuf, vbuf, obuf, vx, ox, vback, oback, ybox, xbox, send_sems, recv_sems, local_sems, y_send, y_recv,
+           x_send, x_recv):
     rows, ry, depth = design.shape
     half = depth // 2
     gx, gy = lax.axis_index("gx"), lax.axis_index("gy")
@@ -114,9 +115,10 @@
     def greet(dev):
         pl.semaphore_signal(barrier, inc=1, device_id=dev, device_id_type=MESH)
 
-    greet(mate)
-    for cond, dev in ((has_xl, xl), (has_xr, xr), (has_yl, yl), (has_yr, yr)):
-        pl.when(cond)(functools.partial(greet, dev))
+    for k in range(1, nx):
+        greet((lax.rem(gx + k, nx), gy))
+    for k in range(1, ny):
+        greet((gx, lax.rem(gy + k, ny)))
 
     own = pl.ds(pl.multiple_of(par * half, 128), half)
     other = pl.ds(pl.multiple_of((1 - par) * half, 128), half)
@@ -131,8 +133,9 @@
     l_mask.start()
     l_sens.start()
 
-    count = 1 + sum(c.astype(jnp.int32) for c in (has_xl, has_xr, has_yl, has_yr))
-    pl.semaphore_wait(barrier, count)
+    l_full = pltpu.make_async_copy(mask, full_mask, local_sems.at[6])
+    l_full.start()
+    pl.semaphore_wait(barrier, nx + ny - 2)
 
     def remote(idx, src, dst, dev):
         return pltpu.make_async_remote_copy(
@@ -290,6 +293,125 @@
     finish(y_o, has_yl, has_yr)
     filter_zy(oback, obj_out, group)
 
+    l_full.wait()
+
+    def along(turn, coord, size, place, box, send, recv):
+        for k in range(1, size):
+            peer = lax.rem(coord + k, size)
+            pltpu.make_async_remote_copy(
+                src_ref=box.at[turn, coord], dst_ref=box.at[turn, coord], send_sem=send.at[turn, k],
+                recv_sem=recv.at[turn, coord], device_id=place(peer), device_id_type=MESH,
+            ).start()
+        for k in range(1, size):
+            peer = lax.rem(coord + k, size)
+            pltpu.make_async_remote_copy(
+                src_ref=box.at[turn, peer], dst_ref=box.at[turn, peer], send_sem=send.at[turn, k],
+                recv_sem=recv.at[turn, peer], device_id=place(peer), device_id_type=MESH,
+            ).wait()
+        out = box[turn, 0]
+        for k in range(1, size):
+            out = out + box[turn, k]
+        return out
+
+    def all_sum(turn, tile):
+        ybox[turn, gy] = tile
+        tile = along(turn, gy, ny, lambda peer: (gx, peer), ybox, y_send, y_recv)
+        xbox[turn, gx] = tile
+        tile = along(turn, gx, nx, lambda peer: (peer, gy), xbox, x_send, x_recv)
+        return jnp.sum(tile, axis=1, keepdims=True)
+
+    part = 32 if ry % 32 == 0 else 8
+    pieces = ry // part
+
+    def fold(x):
+        out = x[0:8]
+        for k in range(1, part // 8):
+            out = out + x[8 * k : 8 * (k + 1)]
+        res = out[:, 0:128]
+        for k in range(1, depth // 128):
+            res = res + out[:, 128 * k : 128 * (k + 1)]
+        return res
+
+    def where_is(i):
+        row = i // pieces
+        start = pl.multiple_of(lax.rem(i, pieces) * part, 8)
+        return row, pl.ds(start, part), pl.ds(RADIUS + start, part)
+
+    def shift_of(lam, grad, swing, cell):
+        up = jnp.maximum(grad, 0.0)
+        down = jnp.maximum(-grad, 0.0)
+        a_two = (0.25 * 1.001) * up + (0.25 * 0.001) * down + 0.25e-05 + lam * ((0.25 * 1.001) * swing)
+        b_two = (0.25 * 0.001) * up + (0.25 * 1.001) * down + 0.25e-05 + lam * ((0.25 * 0.001) * swing)
+        a_root, b_root = jnp.sqrt(a_two), jnp.sqrt(b_two)
+        inv = 1.0 / (a_root + b_root)
+        raw = (0.5 * (b_root - a_root)) * inv
+        low = jnp.maximum(-cell, -move_limit)
+        high = jnp.minimum(1.0 - cell, move_limit)
+        return a_root, b_root, inv, raw, low, high
+
+    def dual_pass(lam, first):
+        def body(i, carry):
+            row, ys, ds = where_is(i)
+            swing = vol_out[row, ys, :]
+            if first:
+                swing = swing * (1 - full_mask[row, ys, :]).astype(jnp.float32)
+                vol_out[row, ys, :] = swing
+            a_root, b_root, inv, raw, low, high = shift_of(lam, obj_out[row, ys, :], swing, dbuf[row, ds, :])
+            point = jnp.clip(raw, low, high)
+            p_one, q_one = (0.25 * 1.001) * swing, (0.25 * 0.001) * swing
+            r_up, r_low = 1.0 / (asym_gap - point), 1.0 / (asym_gap + point)
+            value_p, value_q = p_one * r_up, q_one * r_low
+            ratio = a_root / b_root
+            moved = 0.5 * (ratio * q_one - p_one / ratio) * (inv * inv)
+            change = jnp.where(
+                jnp.logical_and(raw > low, raw < high), (value_p * r_up - value_q * r_low) * moved, 0.0
+            )
+            out = (carry[0] + fold(value_p + value_q), carry[1] + fold(change))
+            if first:
+                out = out + (carry[2] + fold(swing),)
+            return out
+
+        zero = jnp.zeros((8, 128), jnp.float32)
+        return lax.fori_loop(0, rows * pieces, body, (zero,) * (3 if first else 2))
+
+    cells = float(rows * ry * depth)
+    cell_count = cells * nx * ny
+    index = lax.broadcasted_iota(jnp.int32, (8, 128), 0)
+
+    def pack(parts):
+        out = jnp.zeros((8, 128), jnp.float32)
+        for k, one in enumerate(parts):
+            out = jnp.where(index == k, jnp.sum(one, axis=0, keepdims=True), out)
+        return out
+
+    lam = jnp.full((1, 1), 1.0, jnp.float32)
+    offset = None
+    for turn in range(DUAL_ITERS):
+        parts = dual_pass(lam, turn == 0)
+        if turn == 0:
+            phys = phys_out[:, 0:128]
+            for k in range(1, half // 128):
+                phys = phys + phys_out[:, 128 * k : 128 * (k + 1)]
+            base = parts[2] * (0.25 * (1.001 + 0.001) / asym_gap)
+            parts = (parts[0], parts[1], phys - base - volume_share * cells / 1024.0)
+        sums = all_sum(turn, pack(parts))
+        if turn == 0:
+            offset = sums[2:3] / cell_count
+        level = sums[0:1] / cell_count + offset
+        rate = sums[1:2] / cell_count
+        lam = lam * jnp.exp(-level / (lam * rate - 1e-06))
+
+    def last(i, carry):
+        row, ys, ds = where_is(i)
+        cell = dbuf[row, ds, :]
+        raw, low, high = shift_of(lam, obj_out[row, ys, :], vol_out[row, ys, :], cell)[3:]
+        point = cell + jnp.clip(raw, low, high)
+        new_out[row, ys, :] = jnp.where(full_mask[row, ys, :] == 1, cell, point)
+        return carry
+
+    lax.fori_loop(0, rows * pieces, last, 0)
+    lam_out[0, 0] = lam[0, 0]
+
     for one in (r_mask, r_a, r_sens, r_vb, r_ob):
         one.wait_send()
     for two in (r_des, y_v, y_o):
@@ -298,26 +420,32 @@
         sent(two, has_xl, has_xr)
 
 
-def gradients(design, sensitivity, solid_mask):
+def per_device(design, sensitivity, solid_mask):
     rows, ry, depth = design.shape
     half = depth // 2
+    nx, ny = lax.axis_size("gx"), lax.axis_size("gy")
     f32 = jnp.float32
+    block = (rows, ry, depth)
     wide = (rows, ry + 2 * RADIUS, depth)
     tall = (2 * rows + 2 * RADIUS, ry, half)
     strip = (2 * rows, ry, half)
     vmem = pl.BlockSpec(memory_space=pltpu.VMEM)
-    return pl.pallas_call(
+    dma = pltpu.SemaphoreType.DMA
+    new_design, objective_grad, lam = pl.pallas_call(
         kernel,
         out_shape=(
-            jax.ShapeDtypeStruct((rows, ry, depth), f32),
-            jax.ShapeDtypeStruct((rows, ry, depth), f32),
-            jax.ShapeDtypeStruct((8, half), f32),
+            jax.ShapeDtypeStruct(block, f32),
+            jax.ShapeDtypeStruct(block, f32),
+            jax.ShapeDtypeStruct((1, 1), f32),
         ),
         in_specs=[pl.BlockSpec(memory_space=pl.ANY)] * 3,
-        out_specs=(vmem, vmem, vmem),
+        out_specs=(vmem, vmem, pl.BlockSpec(memory_space=pltpu.SMEM)),
         scratch_shapes=[
+            pltpu.VMEM(block, f32),
+            pltpu.VMEM((8, half), f32),
+            pltpu.VMEM(block, jnp.int32),
             pltpu.VMEM(wide, f32),
-            pltpu.VMEM((rows, ry, depth), f32),
+            pltpu.VMEM(block, f32),
             pltpu.VMEM(tall, f32),
             pltpu.VMEM(strip, jnp.int32),
             pltpu.VMEM(strip, f32),
@@ -327,63 +455,21 @@
             pltpu.VMEM(strip, f32),
             pltpu.VMEM(wide, f32),
             pltpu.VMEM(wide, f32),
-            pltpu.SemaphoreType.DMA((COUNT,)),
-            pltpu.SemaphoreType.DMA((COUNT,)),
-            pltpu.SemaphoreType.DMA((6,)),
+            pltpu.VMEM((DUAL_ITERS, ny, 8, 128), f32),
+            pltpu.VMEM((DUAL_ITERS, nx, 8, 128), f32),
+            dma((COUNT,)),
+            dma((COUNT,)),
+            dma((7,)),
+            dma((DUAL_ITERS, ny)),
+            dma((DUAL_ITERS, ny)),
+            dma((DUAL_ITERS, nx)),
+            dma((DUAL_ITERS, nx)),
         ],
         compiler_params=pltpu.CompilerParams(
             collective_id=0, has_side_effects=True, vmem_limit_bytes=56 * 1024 * 1024
         ),
     )(design, sensitivity, solid_mask)
-
-
-def dual_point(lam, design, p_zero, q_zero, p_one, q_one, lower, upper):
-    low = design - asym_gap
-    upp = design + asym_gap
-    a_root = jnp.sqrt(p_zero + lam * p_one)
-    b_root = jnp.sqrt(q_zero + lam * q_one)
-    raw = (a_root * low + b_root * upp) / (a_root + b_root)
-    inside = jnp.logical_and(raw > lower, raw < upper).astype(jnp.float32)
-    point = jnp.clip(raw, lower, upper)
-    value = p_one / (upp - point) + q_one / (point - low)
-    moved = (
-        (upp - low)
-        * (a_root * q_one / (2.0 * b_root) - b_root * p_one / (2.0 * a_root))
-        / (a_root + b_root) ** 2
-    )
-    change = (p_one / (upp - point) ** 2 - q_one / (point - low) ** 2) * inside * moved
-    return (point, value, change)
-
-
-def per_device(design, sensitivity, solid_mask):
-    rows_x, rows_y, depth = design.shape
-    cell_count = float(rows_x * rows_y * depth * lax.axis_size("gx") * lax.axis_size("gy"))
-    objective_grad, volume_grad, phys = gradients(design, sensitivity, solid_mask)
-    free = (1 - solid_mask).astype(jnp.float32)
-    p_zero = 0.25 * (
-        1.001 * jnp.maximum(objective_grad, 0.0) + 0.001 * jnp.maximum(-objective_grad, 0.0) + 1e-05
-    )
-    q_zero = 0.25 * (
-        0.001 * jnp.maximum(objective_grad, 0.0) + 1.001 * jnp.maximum(-objective_grad, 0.0) + 1e-05
-    )
-    p_one = 0.25 * 1.001 * volume_grad * free
-    q_one = 0.25 * 0.001 * volume_grad * free
-    lower = jnp.maximum(0.0, design - move_limit)
-    upper = jnp.minimum(1.0, design + move_limit)
-    base_local = jnp.sum((p_one + q_one) / asym_gap)
-    mass_local = jnp.sum(phys) - volume_share * rows_x * rows_y * depth
-    lam = jnp.float32(1.0)
-    base_total, mass_total = lax.psum((base_local, mass_local), ("gx", "gy"))
-    offset = mass_total / cell_count - base_total / cell_count
-    for turn in range(DUAL_ITERS):
-        point, value, change = dual_point(lam, design, p_zero, q_zero, p_one, q_one, lower, upper)
-        value_total, change_total = lax.psum((jnp.sum(value), jnp.sum(change)), ("gx", "gy"))
-        level = value_total / cell_count + offset
-        rate = change_total / cell_count
-        lam = lam * jnp.exp(-level / (lam * rate - 1e-06))
-    point, value, change = dual_point(lam, design, p_zero, q_zero, p_one, q_one, lower, upper)
-    new_design = jnp.where(solid_mask == 1, design, point)
-    return (new_design, objective_grad, lam)
+    return new_design, objective_grad, lam.reshape(())
 
 
 def solution(mesh):

time: 249 us -> 170 us (0.68)
  blocking collectives: 87.1 us -> 0 us
  Pallas kernels: 129 us -> 163 us
  other arithmetic: 25.1 us -> 0 us
  between operations: 6.37 us -> 2.47 us
  local copies, waits for them, and re-layouts: 1.34 us -> 4.61 us
    psum x2 -> x0, blocking collectives: 87.1 us -> none  [per_device(): lax.psum((jnp.sum(value), jnp.sum(change)), ('gx', 'gy'))]
    pallas_call x1, Pallas kernels: 129 us -> 163 us  [per_device(): pl.pallas_call(kernel, out_shape=(jax.ShapeDtypeStruct(block, f32), jax.S...]
    reduce_sum x3 -> x0, other arithmetic: 17.9 us -> none  [the longest x2 17.3 us: per_device(): jnp.sum(change)]
    select_n x1 -> x0, other arithmetic: 7.17 us -> none  [per_device(): new_design = jnp.where(solid_mask == 1, design, point)]
    unnamed x9 -> x4, local copies, waits for them, and re-layouts: 1.34 us -> 4.61 us
where the time goes in v1:
time: 170 us
  Pallas kernels  163 us (96%)
  local copies, waits for them, and re-layouts  4.61 us (3%)
  between operations  2.47 us (1%)
    pallas_call x1, Pallas kernels, per_device(): pl.pallas_call(kernel, out_shape=(jax.ShapeDtypeStruct(block, f32), jax.S...  163 us
    unnamed x4, local copies, waits for them, and re-layouts  4.61 us

profile of v1, /device:TPU:0, one launch (start us, length us, event | category | flops | bytes accessed | tf_op | source)
XLA Modules:
  0.0 169.8 jit_solution(16618396869725415012)
XLA Ops:
  0.6 162.8 %shard_map.58 = (f32[16,64,512]{2,1,0:T(8,128)}, f32[16,64,512]{2,1,0:T(8,128)}, f32[1,1]{1,0:T(1,128)}) custom-call(f32[16,64,512]{2,1,0:T(8,128)} %design.1, f32[16,64,512]{2,1,0:T(8,128)} %sens.1, s32[16,64,512]{2,1,0:T(8,128)} %mask.1), custom_call_target="tpu_custom_call" | custom-call | tf_op jit(solution)/shard_map/pallas_call | solution.py:434
  163.4 0.0 copy-start
  163.4 3.3 %copy.9 = f32[16,64,512]{2,1,0:T(8,128)} copy(f32[16,64,512]{2,1,0:T(8,128)} %get-tuple-element.12) | data formatting | bytes 4194304
  166.7 0.0 copy-done
  166.7 1.3 copy.10
Async XLA Ops:
  163.4 3.3 %copy-start = (f32[16,64,512]{2,1,0:T(8,128)S(1)}, f32[16,64,512]{2,1,0:T(8,128)}, u32[]{:S(2)}) copy-start(f32[16,64,512]{2,1,0:T(8,128)} %get-tuple-element.13) | copy-start | bytes 6291460

commit v2 on v1

--- a/solution.py
+++ b/solution.py
@@ -37,8 +37,9 @@
     return hi, lo
 
 
-def filter_zy(src, dst, group):
-    rows, wide, depth = src.shape
+def filter_zy(src, dst, group, first=0, rows=None):
+    _, wide, depth = src.shape
+    rows = src.shape[0] if rows is None else rows
     ry = wide - 2 * RADIUS
     jj = lax.broadcasted_iota(jnp.int32, (ry, wide), 0)
     bb = lax.broadcasted_iota(jnp.int32, (ry, wide), 1)
@@ -50,7 +51,7 @@
     def body(g, carry):
         his, los = [], []
         for r in range(group):
-            hi, lo = split2(src[g * group + r])
+            hi, lo = split2(src[first + g * group + r])
             out = jnp.dot(band_y, hi, preferred_element_type=jnp.float32) + jnp.dot(
                 band_y, lo, preferred_element_type=jnp.float32
             )
@@ -63,7 +64,7 @@
         half = group * ry
         total = both[:half] + both[half:]
         for r in range(group):
-            dst[g * group + r] = total[r * ry : (r + 1) * ry]
+            dst[first + g * group + r] = total[r * ry : (r + 1) * ry]
         return carry
 
     lax.fori_loop(0, rows // group, body, 0)
@@ -91,8 +92,10 @@
         emit(i, total)
 
 
-(DES_UP, DES_DN, MASK, SENS, AFLD, A_UP, A_DN, V_UP, V_DN, O_UP, O_DN, VB, OB,
- VY_UP, VY_DN, OY_UP, OY_DN, COUNT) = range(18)
+(DES_UP, DES_DN, MASK, SENS, AFLD, A_UP, A_DN, V_UP, V_DN, O_UP, O_DN, VB,
+ VY_UP, VY_DN, MASK_TWO, LAST) = range(16)
+CHUNKS = 4
+OB, OY_UP, OY_DN, COUNT = LAST, LAST + CHUNKS, LAST + 2 * CHUNKS, LAST + 3 * CHUNKS
 
 
 def kernel(design, sens, mask, new_out, obj_out, lam_out, vol_out, phys_out, full_mask, dbuf, afull, abuf, mbuf,
@@ -169,8 +172,13 @@
 
     r_des = y_pair(DES_UP, DES_DN, design, 0, dbuf)
     begin(r_des, has_yl, has_yr)
-    r_mask = remote(MASK, mask.at[:, :, other], mbuf.at[my_rows], mate)
+    ahead = max(rows // 4, 1)
+    r_mask = remote(MASK, mask.at[pl.ds(0, ahead), :, other], mbuf.at[pl.ds(par * rows, ahead)], mate)
     r_mask.start()
+    r_rest = remote(
+        MASK_TWO, mask.at[pl.ds(ahead, rows - ahead), :, other],
+        mbuf.at[pl.ds(par * rows + ahead, rows - ahead)], mate,
+    )
 
     def zero_y(buf):
         zero = jnp.zeros((rows, RADIUS, depth), jnp.float32)
@@ -205,6 +213,7 @@
     filter_zy(dbuf, afull, group)
     r_a = remote(AFLD, afull.at[:, :, other], abuf.at[pl.ds(RADIUS + par * rows, rows)], mate)
     r_a.start()
+    r_rest.start()
     r_sens = remote(SENS, sens.at[:, :, other], sbuf.at[my_rows], mate)
     r_sens.start()
     l_a = pltpu.make_async_copy(afull.at[:, :, own], abuf.at[pl.ds(RADIUS + par * rows, rows)], local_sems.at[3])
@@ -215,6 +224,7 @@
     begin(x_a, has_xl, has_xr)
     l_mask.wait()
     r_mask.wait_recv()
+    r_rest.wait_recv()
     finish(x_a, has_xl, has_xr)
 
     total_x, total_y = rows * nx, ry * ny
@@ -274,8 +284,15 @@
     begin(x_o, has_xl, has_xr)
     finish(x_o, has_xl, has_xr)
     x_only(obuf, ox)
-    r_ob = remote(OB, ox.at[mate_rows], oback.at[:, mid, own], mate)
-    r_ob.start()
+    chunks = CHUNKS if rows % CHUNKS == 0 else 1
+    step = rows // chunks
+    r_ob = [
+        remote(OB + c, ox.at[pl.ds((1 - par) * rows + c * step, step)],
+               oback.at[pl.ds(c * step, step), mid, own], mate)
+        for c in range(chunks)
+    ]
+    for one in r_ob:
+        one.start()
     l_ob = pltpu.make_async_copy(ox.at[my_rows], oback.at[:, mid, own], local_sems.at[5])
     l_ob.start()
 
@@ -285,13 +302,6 @@
     begin(y_v, has_yl, has_yr)
     finish(y_v, has_yl, has_yr)
     filter_zy(vback, vol_out, group)
-
-    l_ob.wait()
-    r_ob.wait_recv()
-    y_o = y_pair(OY_UP, OY_DN, oback, RADIUS, oback)
-    begin(y_o, has_yl, has_yr)
-    finish(y_o, has_yl, has_yr)
-    filter_zy(oback, obj_out, group)
 
     l_full.wait()
 
@@ -342,27 +352,30 @@
         down = jnp.maximum(-grad, 0.0)
         a_two = (0.25 * 1.001) * up + (0.25 * 0.001) * down + 0.25e-05 + lam * ((0.25 * 1.001) * swing)
         b_two = (0.25 * 0.001) * up + (0.25 * 1.001) * down + 0.25e-05 + lam * ((0.25 * 0.001) * swing)
-        a_root, b_root = jnp.sqrt(a_two), jnp.sqrt(b_two)
-        inv = 1.0 / (a_root + b_root)
+        a_inv, b_inv = lax.rsqrt(a_two), lax.rsqrt(b_two)
+        a_root, b_root = a_two * a_inv, b_two * b_inv
+        inv = pl.reciprocal(a_root + b_root)
         raw = (0.5 * (b_root - a_root)) * inv
         low = jnp.maximum(-cell, -move_limit)
         high = jnp.minimum(1.0 - cell, move_limit)
-        return a_root, b_root, inv, raw, low, high
-
-    def dual_pass(lam, first):
+        return a_root, b_root, a_inv, b_inv, inv, raw, low, high
+
+    def dual_pass(lam, first, begin_at, number, start):
         def body(i, carry):
             row, ys, ds = where_is(i)
             swing = vol_out[row, ys, :]
             if first:
                 swing = swing * (1 - full_mask[row, ys, :]).astype(jnp.float32)
                 vol_out[row, ys, :] = swing
-            a_root, b_root, inv, raw, low, high = shift_of(lam, obj_out[row, ys, :], swing, dbuf[row, ds, :])
+            a_root, b_root, a_inv, b_inv, inv, raw, low, high = shift_of(
+                lam, obj_out[row, ys, :], swing, dbuf[row, ds, :]
+            )
             point = jnp.clip(raw, low, high)
             p_one, q_one = (0.25 * 1.001) * swing, (0.25 * 0.001) * swing
-            r_up, r_low = 1.0 / (asym_gap - point), 1.0 / (asym_gap + point)
+            both = pl.reciprocal(asym_gap * asym_gap - point * point)
+            r_up, r_low = (asym_gap + point) * both, (asym_gap - point) * both
             value_p, value_q = p_one * r_up, q_one * r_low
-            ratio = a_root / b_root
-            moved = 0.5 * (ratio * q_one - p_one / ratio) * (inv * inv)
+            moved = 0.5 * (a_root * b_inv * q_one - b_root * a_inv * p_one) * (inv * inv)
             change = jnp.where(
                 jnp.logical_and(raw > low, raw < high), (value_p * r_up - value_q * r_low) * moved, 0.0
             )
@@ -371,8 +384,7 @@
                 out = out + (carry[2] + fold(swing),)
             return out
 
-        zero = jnp.zeros((8, 128), jnp.float32)
-        return lax.fori_loop(0, rows * pieces, body, (zero,) * (3 if first else 2))
+        return lax.fori_loop(begin_at * pieces, (begin_at + number) * pieces, body, start)
 
     cells = float(rows * ry * depth)
     cell_count = cells * nx * ny
@@ -386,8 +398,25 @@
 
     lam = jnp.full((1, 1), 1.0, jnp.float32)
     offset = None
+    zero = jnp.zeros((8, 128), jnp.float32)
+
+    l_ob.wait()
+    y_o = []
+    parts = (zero,) * 3
+    for c in range(chunks + 1):
+        if c < chunks:
+            r_ob[c].wait_recv()
+            piece = oback.at[pl.ds(c * step, step)]
+            y_o.append(y_pair(OY_UP + c, OY_DN + c, piece, RADIUS, piece))
+            begin(y_o[c], has_yl, has_yr)
+        if c >= 1:
+            finish(y_o[c - 1], has_yl, has_yr)
+            filter_zy(oback, obj_out, step, (c - 1) * step, step)
+            parts = dual_pass(lam, True, (c - 1) * step, step, parts)
+
     for turn in range(DUAL_ITERS):
-        parts = dual_pass(lam, turn == 0)
+        if turn > 0:
+            parts = dual_pass(lam, False, 0, rows, (zero,) * 2)
         if turn == 0:
             phys = phys_out[:, 0:128]
             for k in range(1, half // 128):
@@ -404,7 +433,7 @@
     def last(i, carry):
         row, ys, ds = where_is(i)
         cell = dbuf[row, ds, :]
-        raw, low, high = shift_of(lam, obj_out[row, ys, :], vol_out[row, ys, :], cell)[3:]
+        raw, low, high = shift_of(lam, obj_out[row, ys, :], vol_out[row, ys, :], cell)[5:]
         point = cell + jnp.clip(raw, low, high)
         new_out[row, ys, :] = jnp.where(full_mask[row, ys, :] == 1, cell, point)
         return carry
@@ -412,9 +441,9 @@
     lax.fori_loop(0, rows * pieces, last, 0)
     lam_out[0, 0] = lam[0, 0]
 
-    for one in (r_mask, r_a, r_sens, r_vb, r_ob):
+    for one in (r_mask, r_rest, r_a, r_sens, r_vb, *r_ob):
         one.wait_send()
-    for two in (r_des, y_v, y_o):
+    for two in (r_des, y_v, *y_o):
         sent(two, has_yl, has_yr)
     for two in (x_a, x_v, x_o):
         sent(two, has_xl, has_xr)

time: 170 us -> 157 us (0.924)
  Pallas kernels: 163 us -> 150 us
    pallas_call x1, Pallas kernels: 163 us -> 150 us  [per_device(): pl.pallas_call(kernel, out_shape=(jax.ShapeDtypeStruct(block, f32), jax.S...]
where the time goes in v2:
time: 157 us
  Pallas kernels  150 us (96%)
  local copies, waits for them, and re-layouts  4.61 us (3%)
  between operations  2.47 us (2%)
    pallas_call x1, Pallas kernels, per_device(): pl.pallas_call(kernel, out_shape=(jax.ShapeDtypeStruct(block, f32), jax.S...  150 us
    unnamed x4, local copies, waits for them, and re-layouts  4.61 us

profile of v2, /device:TPU:0, one launch (start us, length us, event | category | flops | bytes accessed | tf_op | source)
XLA Modules:
  0.0 157.0 jit_solution(6977907526803085929)
XLA Ops:
  0.6 149.9 %shard_map.58 = (f32[16,64,512]{2,1,0:T(8,128)}, f32[16,64,512]{2,1,0:T(8,128)}, f32[1,1]{1,0:T(1,128)}) custom-call(f32[16,64,512]{2,1,0:T(8,128)} %design.1, f32[16,64,512]{2,1,0:T(8,128)} %sens.1, s32[16,64,512]{2,1,0:T(8,128)} %mask.1), custom_call_target="tpu_custom_call" | custom-call | tf_op jit(solution)/shard_map/pallas_call | solution.py:463
  150.5 0.0 copy-start
  150.5 3.3 %copy.9 = f32[16,64,512]{2,1,0:T(8,128)} copy(f32[16,64,512]{2,1,0:T(8,128)} %get-tuple-element.12) | data formatting | bytes 4194304
  153.8 0.0 copy-done
  153.8 1.3 copy.10
Async XLA Ops:
  150.5 3.3 %copy-start = (f32[16,64,512]{2,1,0:T(8,128)S(1)}, f32[16,64,512]{2,1,0:T(8,128)}, u32[]{:S(2)}) copy-start(f32[16,64,512]{2,1,0:T(8,128)} %get-tuple-element.13) | copy-start | bytes 6291460

commit v3 on v2

--- a/solution.py
+++ b/solution.py
@@ -94,13 +94,13 @@
 
 (DES_UP, DES_DN, MASK, SENS, AFLD, A_UP, A_DN, V_UP, V_DN, O_UP, O_DN, VB,
  VY_UP, VY_DN, MASK_TWO, LAST) = range(16)
-CHUNKS = 4
+CHUNKS = 8
 OB, OY_UP, OY_DN, COUNT = LAST, LAST + CHUNKS, LAST + 2 * CHUNKS, LAST + 3 * CHUNKS
 
 
-def kernel(design, sens, mask, new_out, obj_out, lam_out, vol_out, phys_out, full_mask, dbuf, afull, abuf, mbuf,
+def kernel(design, sens, mask, new_hbm, obj_hbm, lam_out, new_out, obj_out, vol_out, phys_out, full_mask, dbuf, afull, abuf, mbuf,
            sbuf, vbuf, obuf, vx, ox, vback, oback, ybox, xbox, send_sems, recv_sems, local_sems, y_send, y_recv,
-           x_send, x_recv):
+           x_send, x_recv, obj_sems, new_sems):
     rows, ry, depth = design.shape
     half = depth // 2
     gx, gy = lax.axis_index("gx"), lax.axis_index("gy")
@@ -172,7 +172,7 @@
 
     r_des = y_pair(DES_UP, DES_DN, design, 0, dbuf)
     begin(r_des, has_yl, has_yr)
-    ahead = max(rows // 4, 1)
+    ahead = max(rows // 2, 1)
     r_mask = remote(MASK, mask.at[pl.ds(0, ahead), :, other], mbuf.at[pl.ds(par * rows, ahead)], mate)
     r_mask.start()
     r_rest = remote(
@@ -341,6 +341,10 @@
         for k in range(1, depth // 128):
             res = res + out[:, 128 * k : 128 * (k + 1)]
         return res
+
+    def leave(src, dst, sems, c):
+        some = pl.ds(c * step, step)
+        return pltpu.make_async_copy(src.at[some], dst.at[some], sems.at[c])
 
     def where_is(i):
         row = i // pieces
@@ -412,6 +416,7 @@
         if c >= 1:
             finish(y_o[c - 1], has_yl, has_yr)
             filter_zy(oback, obj_out, step, (c - 1) * step, step)
+            leave(obj_out, obj_hbm, obj_sems, c - 1).start()
             parts = dual_pass(lam, True, (c - 1) * step, step, parts)
 
     for turn in range(DUAL_ITERS):
@@ -438,8 +443,13 @@
         new_out[row, ys, :] = jnp.where(full_mask[row, ys, :] == 1, cell, point)
         return carry
 
-    lax.fori_loop(0, rows * pieces, last, 0)
+    for c in range(chunks):
+        lax.fori_loop(c * step * pieces, (c + 1) * step * pieces, last, 0)
+        leave(new_out, new_hbm, new_sems, c).start()
     lam_out[0, 0] = lam[0, 0]
+    for c in range(chunks):
+        leave(obj_out, obj_hbm, obj_sems, c).wait()
+        leave(new_out, new_hbm, new_sems, c).wait()
 
     for one in (r_mask, r_rest, r_a, r_sens, r_vb, *r_ob):
         one.wait_send()
@@ -458,7 +468,7 @@
     wide = (rows, ry + 2 * RADIUS, depth)
     tall = (2 * rows + 2 * RADIUS, ry, half)
     strip = (2 * rows, ry, half)
-    vmem = pl.BlockSpec(memory_space=pltpu.VMEM)
+    anywhere = pl.BlockSpec(memory_space=pl.ANY)
     dma = pltpu.SemaphoreType.DMA
     new_design, objective_grad, lam = pl.pallas_call(
         kernel,
@@ -467,9 +477,11 @@
             jax.ShapeDtypeStruct(block, f32),
             jax.ShapeDtypeStruct((1, 1), f32),
         ),
-        in_specs=[pl.BlockSpec(memory_space=pl.ANY)] * 3,
-        out_specs=(vmem, vmem, pl.BlockSpec(memory_space=pltpu.SMEM)),
+        in_specs=[anywhere] * 3,
+        out_specs=(anywhere, anywhere, pl.BlockSpec(memory_space=pltpu.SMEM)),
         scratch_shapes=[
+            pltpu.VMEM(block, f32),
+            pltpu.VMEM(block, f32),
             pltpu.VMEM(block, f32),
             pltpu.VMEM((8, half), f32),
             pltpu.VMEM(block, jnp.int32),
@@ -493,6 +505,8 @@
             dma((DUAL_ITERS, ny)),
             dma((DUAL_ITERS, nx)),
             dma((DUAL_ITERS, nx)),
+            dma((CHUNKS,)),
+            dma((CHUNKS,)),
         ],
         compiler_params=pltpu.CompilerParams(
             collective_id=0, has_side_effects=True, vmem_limit_bytes=56 * 1024 * 1024

time: 157 us -> 155 us (0.987)
  Pallas kernels: 150 us -> 148 us
    pallas_call x1, Pallas kernels: 150 us -> 148 us  [per_device(): pl.pallas_call(kernel, out_shape=(jax.ShapeDtypeStruct(block, f32), jax.S...]
where the time goes in v3:
time: 155 us
  Pallas kernels  148 us (95%)
  local copies, waits for them, and re-layouts  4.61 us (3%)
  between operations  2.47 us (2%)
    pallas_call x1, Pallas kernels, per_device(): pl.pallas_call(kernel, out_shape=(jax.ShapeDtypeStruct(block, f32), jax.S...  148 us
    unnamed x4, local copies, waits for them, and re-layouts  4.61 us

profile of v3, /device:TPU:0, one launch (start us, length us, event | category | flops | bytes accessed | tf_op | source)
XLA Modules:
  0.0 155.2 jit_solution(12573402282634387265)
XLA Ops:
  0.6 148.1 %shard_map.58 = (f32[16,64,512]{2,1,0:T(8,128)}, f32[16,64,512]{2,1,0:T(8,128)}, f32[1,1]{1,0:T(1,128)}) custom-call(f32[16,64,512]{2,1,0:T(8,128)} %design.1, f32[16,64,512]{2,1,0:T(8,128)} %sens.1, s32[16,64,512]{2,1,0:T(8,128)} %mask.1), custom_call_target="tpu_custom_call" | custom-call | tf_op jit(solution)/shard_map/pallas_call | solution.py:473
  148.7 0.0 copy-start
  148.7 3.3 %copy.9 = f32[16,64,512]{2,1,0:T(8,128)} copy(f32[16,64,512]{2,1,0:T(8,128)} %get-tuple-element.12) | data formatting | bytes 4194304
  152.0 0.0 copy-done
  152.0 1.3 copy.10
Async XLA Ops:
  148.7 3.3 %copy-start = (f32[16,64,512]{2,1,0:T(8,128)S(1)}, f32[16,64,512]{2,1,0:T(8,128)}, u32[]{:S(2)}) copy-start(f32[16,64,512]{2,1,0:T(8,128)} %get-tuple-element.13) | copy-start | bytes 6291460
